TPU v7x, 32 devices: a whole 2x2x4 slice. The times are simulated.
32 devices in a mesh: gx: 8 (over z, y), gy: 4 (over x, core).
Axes of the slice: x: 2, y: 2, z: 4, core: 2. Of those that a mesh axis runs over, the one named last changes fastest.
Arguments:
- vorticity_grid: float32 [4096, 4096], P(('gx', 'gy')), may hold values from -6 to 6
- forcing_grid: float32 [4096, 4096], P(('gx', 'gy')), may hold values from -12 to 12
- cutoff: int32 [1], replicated, may hold values from 853 to 1365
- forcing_shells: int32 [4], replicated, may hold values from 2 to 127
Outputs:
- lifted_spectrum: float32 [2, 4096, 4096], P(None, ('gx', 'gy'))
- coarse_field: float32 [256, 256], P(('gx', 'gy'))
Inputs may be any that keep to these rules, and one draw needn't show every extreme that they name: Nonlinear modes with an absolute wavenumber index above cutoff are removed.
All inputs are finite; a program needn't handle non-finite values.
Results may differ from a plain program's by a relative error of at most 0.0001.
Values sent between devices are 32-bit elements; how exact they have to be, the bound alone decides.
A program may use at most 128 MiB of HBM per device.

v0:
```python
import math

import jax
import jax.numpy as jnp
from jax import lax
from jax.sharding import PartitionSpec as P

RADIX = 64
LOW = 256
SHELLS = 4


time_step = 0.05
viscosity = 0.05
coarse_ratio = 4.0


def signed_index(index_array, length_of):
    return jnp.where(index_array < length_of // 2, index_array, index_array - length_of)


def pair_tables(first_ids, second_ids, length_of):
    product = first_ids[:, None] * second_ids[None, :] % length_of
    phases = 2.0 * math.pi / length_of * product.astype(jnp.float32)
    factor = 1.0 / math.sqrt(length_of)
    return (jnp.cos(phases) * factor, jnp.sin(phases) * factor)


def contract(pattern, left_side, right_side):
    return jnp.einsum(pattern, left_side, right_side, precision=lax.Precision.HIGHEST)


def complex_table(direction):
    indices = jnp.arange(RADIX, dtype=jnp.int32)
    cos_table, sin_table = pair_tables(indices, indices, RADIX)
    signed_sin = direction * sin_table
    from_real = jnp.stack([cos_table, signed_sin], axis=1)
    from_imag = jnp.stack([-signed_sin, cos_table], axis=1)
    return jnp.stack([from_real, from_imag], axis=0)


def dft_last(values, direction, is_real):
    length_of = values.shape[-1]
    table = complex_table(direction)
    if is_real:
        leading = values.shape[:-1]
        split_values = values.reshape(leading + (RADIX, RADIX))
        first = contract("...ab,adk->d...kb", split_values, table[0])
    else:
        leading = values.shape[1:-1]
        split_values = values.reshape((2,) + leading + (RADIX, RADIX))
        first = contract("c...ab,cadk->d...kb", split_values, table)
    indices = jnp.arange(RADIX, dtype=jnp.int32)
    twiddle_index = indices[:, None] * indices[None, :] % length_of
    twiddle_phase = 2.0 * math.pi / length_of * twiddle_index.astype(jnp.float32)
    twiddle_real = jnp.cos(twiddle_phase)
    twiddle_imag = direction * jnp.sin(twiddle_phase)
    turned = jnp.stack(
        [
            first[0] * twiddle_real - first[1] * twiddle_imag,
            first[0] * twiddle_imag + first[1] * twiddle_real,
        ]
    )
    final = contract("c...kb,cbdj->d...jk", turned, table)
    return final.reshape((2,) + leading + (length_of,))


def rows_to_grid(packed):
    return lax.all_to_all(packed, ("gx", "gy"), split_axis=1, concat_axis=2, tiled=True)


def rows_to_waves(packed):
    return lax.all_to_all(packed, ("gx", "gy"), split_axis=2, concat_axis=1, tiled=True)


def forward(fields):
    field_count = fields.shape[0]
    half = dft_last(fields, -1.0, True)
    moved = rows_to_waves(half.reshape((2 * field_count,) + half.shape[2:]))
    moved = jnp.swapaxes(moved, 1, 2)
    return dft_last(moved.reshape((2, field_count) + moved.shape[1:]), -1.0, False)


def inverse(spectra):
    field_count = spectra.shape[1]
    half = dft_last(spectra, 1.0, False)
    packed = jnp.swapaxes(half.reshape((2 * field_count,) + half.shape[2:]), 1, 2)
    moved = rows_to_grid(packed)
    return dft_last(moved.reshape((2, field_count) + moved.shape[1:]), 1.0, False)


def body(vorticity_grid, forcing_grid, cutoff, forcing_shells):
    row_count = vorticity_grid.shape[0]
    grid_size = vorticity_grid.shape[1]
    device_rank = lax.axis_index("gx") * lax.axis_size("gy") + lax.axis_index("gy")
    device_total = lax.axis_size("gx") * lax.axis_size("gy")
    row_start = device_rank * row_count
    row_ids = row_start + jnp.arange(row_count, dtype=jnp.int32)
    col_ids = jnp.arange(grid_size, dtype=jnp.int32)
    wave_y = signed_index(row_ids, grid_size)[:, None]
    wave_x = signed_index(col_ids, grid_size)[None, :]
    wave_unit = 2.0 * math.pi / grid_size
    deriv_y = (
        jnp.where(row_ids[:, None] == grid_size // 2, 0, wave_y).astype(jnp.float32) * wave_unit
    )
    deriv_x = (
        jnp.where(col_ids[None, :] == grid_size // 2, 0, wave_x).astype(jnp.float32) * wave_unit
    )
    squares = wave_x * wave_x + wave_y * wave_y
    laplace = squares.astype(jnp.float32) * (wave_unit * wave_unit)
    inverse_lap = jnp.where(squares == 0, 0.0, 1.0 / jnp.maximum(laplace, wave_unit * wave_unit))
    dealias = (jnp.abs(wave_x) <= cutoff[0]) & (jnp.abs(wave_y) <= cutoff[0])
    shell_mask = jnp.zeros((row_count, grid_size), dtype=bool)
    for shell_index in range(SHELLS):
        radius = forcing_shells[shell_index]
        shell_mask = shell_mask | (radius * radius <= squares) & (
            squares < (radius + 1) * (radius + 1)
        )
    started = forward(jnp.stack([vorticity_grid, forcing_grid]))
    drive_real = jnp.where(shell_mask, started[0, 1], 0.0)
    drive_imag = jnp.where(shell_mask, started[1, 1], 0.0)
    state_real = started[0, 0]
    state_imag = started[1, 0]

    def tendency(now_real, now_imag):
        stream_real = now_real * inverse_lap
        stream_imag = now_imag * inverse_lap
        speed_real = deriv_x * stream_real - deriv_y * stream_imag
        speed_imag = deriv_x * stream_imag + deriv_y * stream_real
        slope_real = -deriv_y * now_real - deriv_x * now_imag
        slope_imag = -deriv_y * now_imag + deriv_x * now_real
        spectra = jnp.stack(
            [jnp.stack([speed_real, slope_real]), jnp.stack([speed_imag, slope_imag])]
        )
        grids = inverse(spectra)
        advect = grids[0, 0] * grids[0, 1] + grids[1, 0] * grids[1, 1]
        term = forward(advect[None])
        out_real = (
            -jnp.where(dealias, term[0, 0], 0.0) - viscosity * laplace * now_real + drive_real
        )
        out_imag = (
            -jnp.where(dealias, term[1, 0], 0.0) - viscosity * laplace * now_imag + drive_imag
        )
        return (out_real, out_imag)

    earlier_real = state_real
    earlier_imag = state_imag
    first_real, first_imag = tendency(state_real, state_imag)
    second_real, second_imag = tendency(
        state_real + time_step * first_real, state_imag + time_step * first_imag
    )
    state_real = state_real + 0.5 * time_step * (first_real + second_real)
    state_imag = state_imag + 0.5 * time_step * (first_imag + second_imag)
    projected_real = state_real + coarse_ratio * (state_real - earlier_real)
    projected_imag = state_imag + coarse_ratio * (state_imag - earlier_imag)
    half_low = LOW // 2
    low_modes = (
        (wave_x >= -half_low) & (wave_x < half_low) & (wave_y >= -half_low) & (wave_y < half_low)
    )
    lifted_real = jnp.where(low_modes, projected_real, state_real)
    lifted_imag = jnp.where(low_modes, projected_imag, state_imag)
    projected = jnp.stack([projected_real, projected_imag])
    low_columns = jnp.concatenate(
        [projected[:, :, :half_low], projected[:, :, grid_size - half_low :]], axis=2
    )
    block_ids = jnp.arange(LOW, dtype=jnp.int32)
    coarse_rows = LOW // device_total
    every_row = lax.all_gather(low_columns, ("gx", "gy"), axis=1, tiled=True)
    block_low = jnp.concatenate(
        [every_row[:, :half_low], every_row[:, grid_size - half_low :]], axis=1
    )
    own_ids = device_rank * coarse_rows + jnp.arange(coarse_rows, dtype=jnp.int32)
    column_cos, column_sin = pair_tables(block_ids, own_ids, LOW)
    mixed_real = contract("qp,pa->qa", block_low[0], column_cos) - contract(
        "qp,pa->qa", block_low[1], column_sin
    )
    mixed_imag = contract("qp,pa->qa", block_low[0], column_sin) + contract(
        "qp,pa->qa", block_low[1], column_cos
    )
    row_cos, row_sin = pair_tables(block_ids, block_ids, LOW)
    coarse = contract("qa,qb->ab", mixed_real, row_cos) - contract("qa,qb->ab", mixed_imag, row_sin)
    return (jnp.stack([lifted_real, lifted_imag]), coarse)


def solution(mesh):
    placed = (P(("gx", "gy"), None), P(("gx", "gy"), None), P(), P())
    return jax.shard_map(
        body,
        mesh=mesh,
        in_specs=placed,
        out_specs=(P(None, ("gx", "gy"), None), P(("gx", "gy"), None)),
        check_vma=False,
    )
```

profile of v0, /device:TPU:0, one launch (start us, length us, event | category | flops | bytes accessed | tf_op | source)
XLA Modules:
  0.0 1329.7 jit_solution(10226126901157418966)
XLA Ops:
  15.7 6.7 fusion.61
  26.6 12.5 fusion.62
  44.0 18.6 %copy.179 = f32[4,128,4096]{1,0,2:T(4,128)} copy(f32[4,128,4096]{1,2,0:T(8,128)S(1)} %bitcast.399) | data formatting | bytes 16777216 | tf_op jit(solution)/shard_map/reshape;reshape | solution.py:79
  62.6 7.9 all-to-all-start
  70.7 185.6 %all-to-all-done = f32[4,128,4096]{1,0,2:T(4,128)} async-done(((f32[4,128,4096]{1,0,2:T(4,128)}), f32[4,128,4096]{1,0,2:T(4,128)}, u32[]{:S(2)}, u32[]{:S(2)}) %all-to-all-start) | async-done | bytes 8388640 | tf_op jit(solution)/shard_map/all_to_all | solution.py:73
  256.3 7.2 copy.180
  263.5 9.0 copy.181
  272.4 15.8 %fusion.65 = f32[2,2,128,64,64]{2,3,4,1,0:T(8,128)S(1)} fusion(f32[2,2,128,64,64]{2,4,3,1,0:T(8,128)} %bitcast.401, f32[2,64,2,64,1,1]{1,3,2,0,5,4:T(8,128)S(1)} %get-tuple-element.58), kind=kOutput, calls=%fused_computation.112 | convolution fusion | flops 3221225472 | bytes 16842752 | tf_op jit(solution)/shard_map/c...ab,cadk->d...kb/dot_general | solution.py:30
  291.7 12.5 fusion.68
  318.7 8.5 fusion.90
  330.7 12.7 fusion.71
  348.3 17.8 %copy.197 = f32[4,4096,128]{2,0,1:T(4,128)S(1)} copy(f32[4,4096,128]{2,1,0:T(8,128)S(1)} %bitcast.402) | data formatting | bytes 16777216 | tf_op jit(solution)/shard_map/transpose | solution.py:87
  366.1 185.3 %all_to_all.84 = f32[4,4096,128]{2,0,1:T(4,128)S(1)} all-to-all(f32[4,4096,128]{2,0,1:T(4,128)S(1)} %copy.197), channel_id=1, replica_groups=mesh['gx'=8,'gy'=4] {'gx','gy'}, dimensions={1} | all-to-all | bytes 16777216 | tf_op jit(solution)/shard_map/all_to_all | solution.py:69
  555.2 9.0 copy.199
  564.1 15.8 %fusion.74 = f32[2,2,128,64,64]{2,3,4,1,0:T(8,128)S(1)} fusion(f32[2,2,128,64,64]{2,4,3,1,0:T(8,128)} %bitcast.404, f32[1,64,2,64]{1,3,2,0:T(8,128)S(1)} %get-tuple-element.60, f32[1,64,2,64]{1,3,2,0:T(8,128)S(1)} %get-tuple-element.59), kind=kOutput, calls=%fused_computation.115 | convolution fusion | flops 3221241856 | bytes 16842752 | tf_op jit(solution)/shard_map/c...ab,cadk->d...kb/dot_general | solution.py:30
  583.4 12.5 fusion.77
  616.5 16.1 %copy.209 = f32[2,128,4096]{1,0,2:T(2,128)} copy(f32[2,128,4096]{1,2,0:T(8,128)S(1)} %bitcast.412) | data formatting | bytes 8388608 | tf_op jit(solution)/shard_map/reshape;reshape | solution.py:79
  645.7 84.6 %all-to-all-done.2 = f32[2,128,4096]{1,0,2:T(2,128)} async-done(((f32[2,128,4096]{1,0,2:T(2,128)}), f32[2,128,4096]{1,0,2:T(2,128)}, u32[]{:S(2)}, u32[]{:S(2)}) %all-to-all-start.2) | async-done | bytes 4194336 | tf_op jit(solution)/shard_map/all_to_all | solution.py:73
  740.5 8.4 fusion.98
  751.2 6.1 fusion.101
  757.3 10.4 multiply_subtract_fusion.9
  769.3 8.5 fusion.89
  781.6 12.5 fusion.80
  799.0 17.8 %copy.228 = f32[4,4096,128]{2,0,1:T(4,128)S(1)} copy(f32[4,4096,128]{2,1,0:T(8,128)S(1)} %bitcast.405) | data formatting | bytes 16777216 | tf_op jit(solution)/shard_map/transpose | solution.py:87
  816.8 187.4 %all_to_all.85 = f32[4,4096,128]{2,0,1:T(4,128)S(1)} all-to-all(f32[4,4096,128]{2,0,1:T(4,128)S(1)} %copy.228), channel_id=1, replica_groups=mesh['gx'=8,'gy'=4] {'gx','gy'}, dimensions={1} | all-to-all | bytes 16777216 | tf_op jit(solution)/shard_map/all_to_all | solution.py:69
  1008.0 9.0 copy.230
  1017.0 15.8 %fusion.83 = f32[2,2,128,64,64]{2,3,4,1,0:T(8,128)S(1)} fusion(f32[2,2,128,64,64]{2,4,3,1,0:T(8,128)} %bitcast.407, f32[1,64,2,64]{1,3,2,0:T(8,128)S(1)} %get-tuple-element.60, f32[1,64,2,64]{1,3,2,0:T(8,128)S(1)} %get-tuple-element.59), kind=kOutput, calls=%fused_computation.118 | convolution fusion | flops 3221241856 | bytes 16842752 | tf_op jit(solution)/shard_map/c...ab,cadk->d...kb/dot_general | solution.py:30
  1036.5 12.5 fusion.86
  1069.4 16.5 %copy.240 = f32[2,128,4096]{1,0,2:T(2,128)} copy(f32[2,128,4096]{1,2,0:T(8,128)S(1)} %bitcast.415) | data formatting | bytes 8388608 | tf_op jit(solution)/shard_map/reshape;reshape | solution.py:79
  1096.2 87.3 %all-to-all-done.4 = f32[2,128,4096]{1,0,2:T(2,128)} async-done(((f32[2,128,4096]{1,0,2:T(2,128)}), f32[2,128,4096]{1,0,2:T(2,128)}, u32[]{:S(2)}, u32[]{:S(2)}) %all-to-all-start.4) | async-done | bytes 4194336 | tf_op jit(solution)/shard_map/all_to_all | solution.py:73
  1193.6 8.4 fusion.107
  1239.2 75.9 %all-gather.2.cloned.1.call-done = f32[2,4096,256]{1,2,0:T(8,128)} async-done(((f32[2,128,256]{1,2,0:T(8,128)}), f32[2,4096,256]{1,2,0:T(8,128)}) %all-gather.2.cloned.1.call-update) | async-done | bytes 8388624 | tf_op jit(solution)/shard_map/all_gather | solution.py:168
  (117 shorter events, 191.8 us)
Async XLA Ops:
  14.1 1.6 copy-start.5
  62.6 193.7 %all-to-all-start = ((f32[4,128,4096]{1,0,2:T(4,128)}), f32[4,128,4096]{1,0,2:T(4,128)}, u32[]{:S(2)}, u32[]{:S(2)}) async-start(f32[4,128,4096]{1,0,2:T(4,128)} %copy.179), calls=%async_computation | async-start | bytes 16777216 | tf_op jit(solution)/shard_map/all_to_all | solution.py:73
  309.1 4.5 copy-start
  313.6 5.1 copy-start.2
  632.7 4.0 copy-start.10
  632.7 97.7 %all-to-all-start.2 = ((f32[2,128,4096]{1,0,2:T(2,128)}), f32[2,128,4096]{1,0,2:T(2,128)}, u32[]{:S(2)}, u32[]{:S(2)}) async-start(f32[2,128,4096]{1,0,2:T(2,128)} %copy.209), calls=%async_computation.2 | async-start | bytes 8388608 | tf_op jit(solution)/shard_map/all_to_all | solution.py:73
  750.3 0.9 copy-start.9
  751.2 6.1 copy-start.3
  751.2 6.1 copy-start.6
  751.2 6.1 copy-start.7
  757.3 10.4 copy-start.1
  1085.9 97.6 %all-to-all-start.4 = ((f32[2,128,4096]{1,0,2:T(2,128)}), f32[2,128,4096]{1,0,2:T(2,128)}, u32[]{:S(2)}, u32[]{:S(2)}) async-start(f32[2,128,4096]{1,0,2:T(2,128)} %copy.240), calls=%async_computation.4 | async-start | bytes 8388608 | tf_op jit(solution)/shard_map/all_to_all | solution.py:73
  1089.8 225.3 %all-gather.2.cloned.1.call-start = ((), (), s32[]{:S(2)}) async-start(), calls=%async_computation.5 | async-start | bytes 8650752 | tf_op jit(solution)/shard_map/all_gather | solution.py:168
  1210.1 3.1 slice-start
  1210.7 3.0 slice-start.1
  1211.9 2.4 copy-start.4
  1225.0 1.7 copy-start.8
Sparse Core Ops, SparseCore 0:
  1225.9 89.2 all-gather.1
where the time goes:
time: 1340 us; the launch traced here: 1330 us
  waiting for transfers between devices  434 us (32%)
  blocking collectives  373 us (28%)
  local copies, waits for them, and re-layouts  214 us (16%)
  matrix products  202 us (15%)
  other arithmetic  67.4 us (5%)
  between operations  23.3 us (2%)
  starting transfers between devices  15.8 us (1%)
    all_to_all x2, blocking collectives, rows_to_grid(): lax.all_to_all(packed, ('gx', 'gy'), split_axis=1, concat_axis=2, tiled=T...  373 us
    all_to_all x3, waiting for transfers between devices, rows_to_waves(): lax.all_to_all(packed, ('gx', 'gy'), split_axis=2, concat_axis=1, tiled=T...  358 us
    dot_general x26, matrix products, contract(): jnp.einsum(pattern, left_side, right_side, precision=lax.Precision.HIGHEST)  202 us
    all_gather x1, waiting for transfers between devices, body(): every_row = lax.all_gather(low_columns, ('gx', 'gy'), axis=1, tiled=True)  75.9 us
    another operation x3, local copies, waits for them, and re-layouts, forward(): moved = rows_to_waves(half.reshape((2 * field_count,) + half.shape[2:]))  51.3 us
    all_to_all x6, local copies, waits for them, and re-layouts, rows_to_waves(): lax.all_to_all(packed, ('gx', 'gy'), split_axis=2, concat_axis=1, tiled=T...  36.4 us
    transpose x2, local copies, waits for them, and re-layouts, inverse(): jnp.swapaxes(half.reshape((2 * field_count,) + half.shape[2:]), 1, 2)  35.6 us
    transpose x8, local copies, waits for them, and re-layouts, contract(): jnp.einsum(pattern, left_side, right_side, precision=lax.Precision.HIGHEST)  34 us
  transfers between devices with their start and end apart: 4, of which 4 were waited for; matrix products, arithmetic and copies ran while one was open for 1% of the time, Pallas kernels for 0%

commit v1 on v0

v1 whole, which is shorter than its diff:
```python
import math

import jax
import jax.numpy as jnp
import numpy as np
from jax import lax
from jax.sharding import PartitionSpec as P

LOW = 256
SHELLS = 4
AXES = ("gx", "gy")

time_step = 0.05
viscosity = 0.05
coarse_ratio = 4.0


def contract(pattern, left_side, right_side):
    return jnp.einsum(pattern, left_side, right_side, precision=lax.Precision.HIGH)


def turn(product, length_of):
    phases = 2.0 * np.pi / length_of * (product % length_of)
    return np.cos(phases), np.sin(phases)


def rotation(cos_part, sin_part, axes):
    pairs = np.stack([np.stack([cos_part, -sin_part]), np.stack([sin_part, cos_part])])
    return np.moveaxis(pairs, (0, 1), axes).astype(np.float32)


def wave_tables(grid, total, rows):
    A = max(64, total)
    B = grid // A
    half = B // 2
    scale = 1.0 / math.sqrt(grid)
    k, a = np.arange(A), np.arange(A)
    b, j = np.arange(B), np.arange(half)
    out = {"A": A, "B": B, "half": half}
    cos_t, sin_t = turn(k[:, None] * a[None, :], A)
    out["y1"] = np.stack([cos_t, -sin_t], 1).astype(np.float32)
    ky = k[:, None] + A * j[None, :]
    cos_t, sin_t = turn(ky[:, :, None] * b, grid)
    y2 = rotation(cos_t * scale, -sin_t * scale, (1, 3))
    plain = y2.copy()
    y2[0, 1, 0, 0, :] = scale * (-1.0) ** b
    y2[0, 1, 0, 1, :] = 0.0
    out["y2"], out["y2_plain"] = y2, plain
    weight = np.where(ky == 0, 1.0, 2.0)[:, :, None] * scale
    cos_t, sin_t, weight = (t.swapaxes(1, 2) for t in (cos_t, sin_t, weight))
    iy = rotation(cos_t * weight, sin_t * weight, (1, 3))
    slope = (ky * (2.0 * np.pi / grid))[:, None, :] * weight
    iyd = rotation(-sin_t * slope, cos_t * slope, (1, 3))
    iy[0, 0, :, 1, 0] = scale * (-1.0) ** b
    iy[0, 1, :, 1, 0] = 0.0
    out["iy"], out["iyd"] = iy, iyd
    cos_t, sin_t = turn(a[:, None] * k[None, :], A)
    out["iy1"] = np.stack([cos_t, -sin_t], 2).astype(np.float32)
    p, s = np.arange(total), np.arange(total)
    q, lane = np.arange(rows), np.arange(rows)
    cos_t, sin_t = turn(p[:, None] * s[None, :], total)
    out["x1"] = rotation(cos_t * scale, -sin_t * scale, (1, 3))
    out["ix1"] = rotation(cos_t.T * scale, sin_t.T * scale, (1, 3))
    cos_t, sin_t = turn(q[:, None] * lane[None, :], rows)
    out["x2"] = rotation(cos_t.T, -sin_t.T, (2, 0))
    out["ix2"] = rotation(cos_t, sin_t, (2, 0))
    cos_t, sin_t = turn(p[:, None] * lane[None, :], grid)
    out["tw"] = np.stack([cos_t, sin_t]).astype(np.float32)
    return out


def body(vorticity_grid, forcing_grid, cutoff, forcing_shells):
    rows, grid = vorticity_grid.shape
    total = lax.axis_size("gx") * lax.axis_size("gy")
    rank = lax.axis_index("gx") * lax.axis_size("gy") + lax.axis_index("gy")
    tables = wave_tables(grid, total, rows)
    A, B, half = tables["A"], tables["B"], tables["half"]
    local = A // total
    half_low = LOW // 2
    kept = (grid // 3) // A + 1
    driven = -(-half_low // A)
    unit = 2.0 * math.pi / grid

    def exchange(values):
        return lax.all_to_all(values, AXES, split_axis=0, concat_axis=0, tiled=True)

    def forward_y(fields, table):
        first = contract("kda,abx->kdbx", tables["y1"], fields)
        second = contract("kdjcb,kcbx->kdjx", table, first)
        return second.reshape((total, local) + second.shape[1:])

    def inverse_y(waves, table):
        waves = waves.reshape((A,) + waves.shape[2:])
        first = contract("kdbcj,kcjx->kdbx", table[..., : waves.shape[2]], waves)
        return contract("akd,kdbx->abx", tables["iy1"], first)

    def twiddle(values, direction):
        cos_t = tables["tw"][0][:, None, None, :]
        sin_t = direction * tables["tw"][1][:, None, None, :]
        real, imag = values[:, :, 0], values[:, :, 1]
        return jnp.stack([real * cos_t - imag * sin_t, real * sin_t + imag * cos_t], 2)

    def forward_x(waves):
        first = contract("pdsc,skcjl->pkdjl", tables["x1"], waves)
        return contract("pkcjl,cldq->pkdjq", twiddle(first, -1.0), tables["x2"])

    def inverse_x(waves):
        first = contract("pkcjq,cqdl->pkdjl", waves, tables["ix2"])
        return contract("sdpc,pkcjl->skdjl", tables["ix1"], twiddle(first, 1.0))

    p_ids = jnp.arange(total, dtype=jnp.int32)[:, None, None, None]
    q_ids = jnp.arange(rows, dtype=jnp.int32)[None, None, None, :]
    k_ids = (rank * local + jnp.arange(local, dtype=jnp.int32))[None, :, None, None]
    j_ids = jnp.arange(half, dtype=jnp.int32)[None, None, :, None]
    kx_ids = p_ids + total * q_ids
    wave_x = jnp.where(kx_ids < grid // 2, kx_ids, kx_ids - grid)
    deriv_x = jnp.where(kx_ids == grid // 2, 0, wave_x).astype(jnp.float32) * unit
    wave_y = k_ids + A * j_ids
    nyquist_y = jnp.full((1, 1, 1, 1), -(grid // 2), jnp.int32)
    origin = (k_ids == 0) & (j_ids == 0)

    def laplacian(rows_y):
        return (wave_x * wave_x + rows_y * rows_y).astype(jnp.float32) * (unit * unit)

    def inverse_laplacian(rows_y):
        squares = wave_x * wave_x + rows_y * rows_y
        lap = squares.astype(jnp.float32) * (unit * unit)
        return jnp.where(squares == 0, 0.0, 1.0 / jnp.maximum(lap, unit * unit))

    def slope_x(pair):
        return (-deriv_x * pair[1], deriv_x * pair[0])

    def packed(main, extra):
        real, imag = main
        if extra is not None:
            real = jnp.where(origin, real - extra[1], real)
            imag = jnp.where(origin, imag + extra[0], imag)
        return jnp.stack([real, imag], 2)

    turned = vorticity_grid.T.reshape(A, B, rows)
    start_half = forward_y(turned, tables["y2"])
    force_half = forward_y(
        forcing_grid.T.reshape(A, B, rows), tables["y2_plain"][:, :, :driven]
    )
    moved = exchange(jnp.concatenate([start_half, force_half], 3))
    spectra = forward_x(moved)
    state = (spectra[:, :, 0, :half], spectra[:, :, 1, :half])
    squares = (wave_x * wave_x + wave_y * wave_y)[:, :, :driven]
    shell = jnp.zeros(squares.shape, bool)
    for index in range(SHELLS):
        radius = forcing_shells[index]
        shell = shell | ((radius * radius <= squares) & (squares < (radius + 1) * (radius + 1)))
    drive = tuple(jnp.where(shell, spectra[:, :, c, half:], 0.0) for c in (0, 1))

    def mirrored(natural):
        return jnp.roll(jnp.flip(natural, -1), 1, -1)

    zero_real, zero_imag = state[0][:, 0, 0].T.reshape(grid), state[1][:, 0, 0].T.reshape(grid)
    back_real, back_imag = mirrored(zero_real), -mirrored(zero_imag)
    own_real, own_imag = 0.5 * (zero_real + back_real), 0.5 * (zero_imag + back_imag)
    nyq_real, nyq_imag = 0.5 * (zero_imag - back_imag), -0.5 * (zero_real - back_real)

    def laid(natural):
        return natural.reshape(rows, total).T[:, None, None, :]

    state = tuple(
        jnp.where(origin, laid(own), part) for own, part in zip((own_real, own_imag), state)
    )
    extra = (laid(nyq_real), laid(nyq_imag))
    lap, inv_lap = laplacian(wave_y), inverse_laplacian(wave_y)
    lap_n, inv_lap_n = laplacian(nyquist_y), inverse_laplacian(nyquist_y)
    dealias = ((jnp.abs(wave_x) <= cutoff[0]) & (jnp.abs(wave_y) <= cutoff[0]))[:, :, :kept]

    def widened(part, count):
        return jnp.pad(part, ((0, 0), (0, 0), (0, count - part.shape[2]), (0, 0)))

    drive_kept = tuple(widened(part, kept) for part in drive)

    def product(psi, psi_x, vort, vort_x):
        speed_u = inverse_y(psi, tables["iyd"])
        slope_wx = inverse_y(vort_x, tables["iy"])
        speed_v = -inverse_y(psi_x, tables["iy"])
        slope_wy = inverse_y(vort, tables["iyd"])
        advect = speed_u * slope_wx + speed_v * slope_wy
        term = forward_x(exchange(forward_y(advect, tables["y2_plain"][:, :, :kept])))
        return tuple(
            drive_kept[c] - jnp.where(dealias, term[:, :, c], 0.0) for c in (0, 1)
        )

    psi = tuple(inv_lap * part for part in state)
    psi_extra = tuple(inv_lap_n * part for part in extra)
    outgoing = jnp.concatenate(
        [
            packed(psi, psi_extra),
            packed(slope_x(psi), slope_x(psi_extra)),
            packed(slope_x(state), slope_x(extra)),
        ],
        3,
    )
    arrived = exchange(inverse_x(outgoing))
    psi_half = arrived[:, :, :, :half]
    psi_x_half = arrived[:, :, :, half : 2 * half]
    vort_x_half = arrived[:, :, :, 2 * half :]
    first = product(psi_half, psi_x_half, start_half, vort_x_half)

    moved_on = tuple(
        part - time_step * viscosity * lap * part + time_step * widened(term, half)
        for part, term in zip(state, first)
    )
    moved_extra = tuple(part - time_step * viscosity * lap_n * part for part in extra)
    psi_kept = tuple(time_step * inv_lap[:, :, :kept] * term for term in first)
    outgoing = jnp.concatenate(
        [
            packed(moved_on, moved_extra),
            packed(slope_x(moved_on), slope_x(moved_extra)),
            jnp.stack(psi_kept, 2),
            jnp.stack(slope_x(psi_kept), 2),
        ],
        3,
    )
    arrived = exchange(inverse_x(outgoing))

    def added(whole, local_part, part):
        part = jnp.pad(part, ((0, 0), (0, 0), (0, 0), (0, half - kept), (0, 0)))
        return whole - time_step * viscosity * local_part + part

    second = product(
        added(psi_half, start_half, arrived[:, :, :, 2 * half : 2 * half + kept]),
        added(psi_x_half, vort_x_half, arrived[:, :, :, 2 * half + kept :]),
        arrived[:, :, :, :half],
        arrived[:, :, :, half : 2 * half],
    )

    def stepped(part, ahead, lap_of, terms):
        linear = -viscosity * lap_of * (part + ahead)
        return part + 0.5 * time_step * (linear if terms is None else linear + terms)

    final = tuple(
        stepped(part, ahead, lap, widened(one + two, half))
        for part, ahead, one, two in zip(state, moved_on, first, second)
    )
    final_extra = tuple(
        stepped(part, ahead, lap_n, None) for part, ahead in zip(extra, moved_extra)
    )
    projected = tuple(new + coarse_ratio * (new - old) for new, old in zip(final, state))

    def lifted(signed_x, signed_y):
        low = (
            (signed_x >= -half_low)
            & (signed_x < half_low)
            & (signed_y >= -half_low)
            & (signed_y < half_low)
        )
        return jnp.stack(
            [jnp.where(low, ahead, now) for ahead, now in zip(projected, final)], 2
        )

    straight = lifted(wave_x, wave_y)
    mirror = lifted(-wave_x, -wave_y)
    nyquist = jnp.stack([part[:, 0] for part in final_extra], 1)[:, None]
    flipped = jnp.flip(mirror, 3)
    shifted = jnp.concatenate(
        [jnp.broadcast_to(nyquist, flipped[:, :, :, :1].shape), flipped[:, :, :, :-1]], 3
    )
    flipped = jnp.where((k_ids == 0)[:, :, None], shifted, flipped)
    whole = jnp.concatenate([straight, flipped], 3)
    sent = whole.transpose(3, 1, 2, 0, 4)
    if rows >= A:
        sent = sent.reshape(total, rows // A, local, 2, total, rows)
        got = exchange(sent)
        sources = got.reshape(total, rows // A, local, 2, total, rows)
        placed = sources.transpose(3, 1, 0, 2, 5, 4).reshape(2, rows, grid)
        back = jnp.roll(
            jnp.flip(placed.reshape(2, rows // A, A, grid), 2), 1, 2
        ).reshape(2, rows, grid)
    else:
        parts = A // rows
        sent = jnp.broadcast_to(sent[:, None], (B, parts) + sent.shape[1:])
        block = exchange(sent.reshape((total,) + sent.shape[2:])).reshape(A, 2, total, rows)
        block = block.transpose(1, 0, 3, 2).reshape(2, A, grid)
        start = (rank % parts) * rows
        placed = lax.dynamic_slice_in_dim(block, start, rows, 1)
        turned_block = jnp.roll(jnp.flip(block, 1), 1, 1)
        back = lax.dynamic_slice_in_dim(turned_block, start, rows, 1)
    back = mirrored(back)
    back = jnp.stack([back[0], -back[1]])
    spectrum = jnp.where(rank >= total // 2, back, placed)

    own = LOW // total
    block_ids = np.arange(LOW)
    col_cos, col_sin = (t.astype(np.float32) / 16.0 for t in turn(block_ids[:, None] * block_ids, LOW))
    low = jnp.concatenate([spectrum[:, :, :half_low], spectrum[:, :, grid - half_low :]], 2)
    column = np.stack([np.stack([col_cos, col_sin]), np.stack([-col_sin, col_cos])])
    mixed = contract("cqp,cdpa->dqa", low, column)
    mixed = mixed.reshape(2, rows, total, own).transpose(2, 0, 1, 3)
    mixed = exchange(mixed)
    count = -(-half_low // rows)
    mixed = jnp.concatenate([mixed[:count], mixed[total - count :]], 0)
    if rows * count != half_low:
        first_rows = mixed[:count].transpose(1, 0, 2, 3).reshape(2, count * rows, own)[:, :half_low]
        last_rows = mixed[count:].transpose(1, 0, 2, 3).reshape(2, count * rows, own)[:, -half_low:]
        mixed = jnp.concatenate([first_rows, last_rows], 1)
    else:
        mixed = mixed.transpose(1, 0, 2, 3).reshape(2, LOW, own)
    row_table = np.stack([col_cos, -col_sin])
    coarse = contract("cqa,cqb->ab", mixed, row_table)
    return (spectrum, coarse)


def solution(mesh):
    placed = (P(AXES, None), P(AXES, None), P(), P())
    return jax.shard_map(
        body,
        mesh=mesh,
        in_specs=placed,
        out_specs=(P(None, AXES, None), P(AXES, None)),
        check_vma=False,
    )
```

time: 1340 us -> 894 us (0.67)
  blocking collectives: 373 us -> 174 us
  waiting for transfers between devices: 434 us -> 327 us
  matrix products: 202 us -> 128 us
  local copies, waits for them, and re-layouts: 214 us -> 180 us
  other arithmetic: 67.4 us -> 37.9 us
    all_to_all x2, blocking collectives: 373 us -> 174 us  [exchange(): return lax.all_to_all(values, AXES, split_axis=0, concat_axis=0, tiled=True)]
    all_gather x1 -> x0, waiting for transfers between devices: 75.9 us -> none  [body(): every_row = lax.all_gather(low_columns, ('gx', 'gy'), axis=1, tiled=True)]
    dot_general x26 -> x36, matrix products: 202 us -> 128 us  [contract(): jnp.einsum(pattern, left_side, right_side, precision=lax.Precision.HIGH)]
    all_to_all x10 -> x0, local copies, waits for them, and re-layouts: 61.9 us -> none  [the longest x6 36.4 us: rows_to_waves(): lax.all_to_all(packed, ('gx', 'gy'), split_axis=2, concat_axis=1, tiled=T...]
    unnamed x29 -> x184, local copies, waits for them, and re-layouts: 14.1 us -> 67.2 us
    another operation x5 -> x1, local copies, waits for them, and re-layouts: 55 us -> 13 us  [body(): placed.reshape(2, rows // A, A, grid)]
    transpose x10 -> x8, local copies, waits for them, and re-layouts: 69.6 us -> 32.5 us  [the longest x3 21.7 us: contract(): jnp.einsum(pattern, left_side, right_side, precision=lax.Precision.HIGH)]
    sub x13 -> x5, other arithmetic: 34.7 us -> 3.08 us  [twiddle(): real * cos_t - imag * sin_t]
  transfers between devices with their start and end apart: 4 -> 5, of which waited for: 4 -> 5; matrix products, arithmetic and copies ran while one was open for 1% -> 2% of each run, Pallas kernels for 0% -> 0%
where the time goes in v1:
time: 894 us; the launch traced here: 879 us
  waiting for transfers between devices  327 us (37%)
  local copies, waits for them, and re-layouts  180 us (20%)
  blocking collectives  174 us (19%)
  matrix products  128 us (14%)
  other arithmetic  37.9 us (4%)
  starting transfers between devices  22.3 us (2%)
  between operations  10.7 us (1%)
    all_to_all x5, waiting for transfers between devices, exchange(): return lax.all_to_all(values, AXES, split_axis=0, concat_axis=0, tiled=True)  327 us
    all_to_all x2, blocking collectives, exchange(): return lax.all_to_all(values, AXES, split_axis=0, concat_axis=0, tiled=True)  174 us
    dot_general x36, matrix products, contract(): jnp.einsum(pattern, left_side, right_side, precision=lax.Precision.HIGH)  128 us
    unnamed x184, local copies, waits for them, and re-layouts  67.2 us
    slice x3, local copies, waits for them, and re-layouts, body(): jnp.roll(jnp.flip(placed.reshape(2, rows // A, A, grid), 2), 1, 2)  24 us
    all_to_all x5, starting transfers between devices, exchange(): return lax.all_to_all(values, AXES, split_axis=0, concat_axis=0, tiled=True)  22.3 us
    transpose x3, local copies, waits for them, and re-layouts, contract(): jnp.einsum(pattern, left_side, right_side, precision=lax.Precision.HIGH)  21.7 us
  transfers between devices with their start and end apart: 5, of which 5 were waited for; matrix products, arithmetic and copies ran while one was open for 2% of the time, Pallas kernels for 0%

profile of v1, /device:TPU:0, one launch (start us, length us, event | category | flops | bytes accessed | tf_op | source)
XLA Modules:
  0.0 879.5 jit_solution(2165284268286502760)
XLA Ops:
  5.5 4.5 convolution_bitcast_fusion.11
  12.9 4.3 fusion.14
  17.3 4.2 fusion.12
  24.3 7.4 all-to-all-start
  33.2 50.0 %all-to-all-done = f32[32,2,2,34,128]{4,2,3,1,0:T(2,128)} async-done(((f32[32,2,2,34,128]{4,2,3,1,0:T(2,128)}), f32[32,2,2,34,128]{4,2,3,1,0:T(2,128)}, u32[]{:S(2)}, u32[]{:S(2)}) %all-to-all-start) | async-done | bytes 2228256 | tf_op jit(solution)/shard_map/all_to_all | solution.py:85
  104.7 5.9 fusion.38
  112.7 7.9 fusion.41
  120.6 10.2 %copy.127 = f32[32,2,2,96,128]{4,2,3,1,0:T(2,128)} copy(f32[32,2,2,96,128]{4,0,2,3,1:T(8,128)} %fusion.41) | data formatting | bytes 12582912 | tf_op jit(solution)/shard_map/sdpc,pkcjl->skdjl/transpose | solution.py:19
  130.9 4.3 all-to-all-start.1
  135.1 5.3 convolution_bitcast_fusion.6
  140.4 4.9 fusion.24
  145.3 129.5 %all-to-all-done.1 = f32[32,2,2,96,128]{4,2,3,1,0:T(2,128)} async-done(((f32[32,2,2,96,128]{4,2,3,1,0:T(2,128)}), f32[32,2,2,96,128]{4,2,3,1,0:T(2,128)}, u32[]{:S(2)}, u32[]{:S(2)}) %all-to-all-start.1) | async-done | bytes 6291488 | tf_op jit(solution)/shard_map/all_to_all | solution.py:85
  293.5 4.0 fusion.28
  308.9 4.5 fusion.10
  334.2 18.8 %all-to-all-done.2 = f32[32,2,2,22,128]{4,2,3,1,0:T(2,128)S(1)} async-done(((f32[32,2,2,22,128]{4,2,3,1,0:T(2,128)}), f32[32,2,2,22,128]{4,2,3,1,0:T(2,128)S(1)}, u32[]{:S(2)}, u32[]{:S(2)}) %all-to-all-start.2) | async-done | bytes 1441824 | tf_op jit(solution)/shard_map/all_to_all | solution.py:85
  367.6 8.8 fusion.35
  376.3 11.3 %copy.141 = f32[32,2,2,108,128]{4,2,3,1,0:T(2,128)} copy(f32[32,2,2,108,128]{4,0,2,3,1:T(8,128)} %fusion.35) | data formatting | bytes 14155776 | tf_op jit(solution)/shard_map/sdpc,pkcjl->skdjl/transpose | solution.py:19
  387.7 159.0 %all_to_all.35 = f32[32,2,2,108,128]{4,2,3,1,0:T(2,128)S(1)} all-to-all(f32[32,2,2,108,128]{4,2,3,1,0:T(2,128)} %copy.141), channel_id=1, replica_groups=mesh['gx'=8,'gy'=4] {'gx','gy'}, dimensions={0} | all-to-all | bytes 14155776 | tf_op jit(solution)/shard_map/all_to_all | solution.py:85
  577.5 4.0 convolution_bitcast_fusion.3
  587.1 4.4 fusion.8
  597.2 34.8 %all-to-all-done.4 = f32[32,2,2,22,128]{4,2,3,1,0:T(2,128)S(1)} async-done(((f32[32,2,2,22,128]{4,2,3,1,0:T(2,128)}), f32[32,2,2,22,128]{4,2,3,1,0:T(2,128)S(1)}, u32[]{:S(2)}, u32[]{:S(2)}) %all-to-all-start.4) | async-done | bytes 1441824 | tf_op jit(solution)/shard_map/all_to_all | solution.py:85
  645.3 3.9 rev.11
  652.1 4.4 copy.154
  656.5 4.0 all-to-all-start.5
  660.5 93.7 %all-to-all-done.5 = f32[32,2,2,2,32,128]{5,4,3,2,1,0:T(8,128)} async-done(((f32[32,2,2,2,32,128]{5,4,3,2,1,0:T(8,128)}), f32[32,2,2,2,32,128]{5,4,3,2,1,0:T(8,128)}, u32[]{:S(2)}, u32[]{:S(2)}) %all-to-all-start.5) | async-done | bytes 4194336 | tf_op jit(solution)/shard_map/all_to_all | solution.py:85
  754.2 10.6 %copy.155 = f32[2,2,32,2,128,32]{5,4,3,2,1,0:T(8,128)} copy(f32[2,2,32,2,128,32]{4,5,0,3,1,2:T(8,128)} %bitcast.189) | data formatting | bytes 8388608 | tf_op jit(solution)/shard_map/transpose | solution.py:272
  764.8 13.0 %reshape_reshape.3 = f32[2,2,64,4096]{3,2,1,0:T(8,128)} reshape(f32[2,2,32,2,128,32]{5,4,3,2,1,0:T(8,128)} %copy.155) | data formatting | bytes 8388608 | tf_op jit(solution)/shard_map/reshape;reshape | solution.py:274
  777.8 4.8 slice.265
  783.7 18.1 %slice.217 = f32[2,2,63,4096]{3,2,1,0:T(8,128)} reverse(f32[2,2,63,4096]{3,2,1,0:T(8,128)} %slice.265), dimensions={2} | reverse | bytes 8257536 | tf_op jit(solution)/shard_map/jit(_roll_static)/slice | solution.py:273
  807.8 13.0 %reshape.575 = f32[2,128,4096]{2,1,0:T(8,128)} reshape(f32[2,2,32,2,128,32]{5,4,3,2,1,0:T(8,128)} %copy.155) | data formatting | bytes 8388608 | tf_op jit(solution)/shard_map/reshape | solution.py:272
  820.9 34.3 %reverse.11 = f32[2,128,4096]{2,1,0:T(8,128)} reverse(f32[2,128,4096]{2,1,0:T(8,128)} %bitcast.476), dimensions={2} | reverse | bytes 8388608
  863.9 14.5 %all_to_all.36 = f32[32,2,128,8]{2,3,1,0:T(8,128)S(1)} all-to-all(f32[32,2,128,8]{2,3,1,0:T(8,128)S(1)} %copy.158), channel_id=1, replica_groups=mesh['gx'=8,'gy'=4] {'gx','gy'}, dimensions={0} | all-to-all | bytes 524288 | tf_op jit(solution)/shard_map/all_to_all | solution.py:85
  (288 shorter events, 166.2 us)
Async XLA Ops:
  12.9 4.4 copy-start.56
  24.2 59.0 %copy-start.37 = (f32[32,2,32,2,1,1]{2,0,3,1,5,4:T(8,128)S(1)}, f32[32,2,32,2,1,1]{2,0,3,1,5,4:T(8,128)}, u32[]{:S(2)}) copy-start(f32[32,2,32,2,1,1]{2,0,3,1,5,4:T(8,128)} %constant.147) | copy-start | bytes 49156
  24.3 59.0 %all-to-all-start = ((f32[32,2,2,34,128]{4,2,3,1,0:T(2,128)}), f32[32,2,2,34,128]{4,2,3,1,0:T(2,128)}, u32[]{:S(2)}, u32[]{:S(2)}) async-start(f32[32,2,2,34,128]{4,2,3,1,0:T(2,128)} %copy.111), calls=%async_computation | async-start | bytes 4456448 | tf_op jit(solution)/shard_map/all_to_all | solution.py:85
  31.7 54.4 %copy-start.41 = (f32[32,128]{1,0:T(8,128)S(1)}, f32[32,128]{1,0:T(8,128)}, u32[]{:S(2)}) copy-start(f32[32,128]{1,0:T(8,128)} %constant.143) | copy-start | bytes 49156
  31.7 54.4 %copy-start.58 = (f32[32,128]{1,0:T(8,128)S(1)}, f32[32,128]{1,0:T(8,128)}, u32[]{:S(2)}) copy-start(f32[32,128]{1,0:T(8,128)} %constant.144) | copy-start | bytes 49156
  32.4 67.7 %copy-start.76 = (s32[128]{0:T(128)}, s32[128]{0:T(128)S(1)}, u32[]{:S(2)}) copy-start(s32[128]{0:T(128)S(1)} %iota_multiply_fusion.1) | copy-start | bytes 1540
  32.4 54.0 %copy-start.82 = (pred[2]{0:T(512)(128)(4,1)}, pred[2]{0:T(512)(128)(4,1)S(1)}, u32[]{:S(2)}) copy-start(pred[2]{0:T(512)(128)(4,1)S(1)} %broadcast_compare_fusion) | copy-start | bytes 10
  32.6 68.3 %copy-start.72 = (s32[2,32]{1,0:T(2,128)}, s32[2,32]{1,0:T(2,128)S(1)}, u32[]{:S(2)}) copy-start(s32[2,32]{1,0:T(2,128)S(1)} %add_multiply_fusion.2) | copy-start | bytes 772
  33.2 67.6 %copy-start.74 = (pred[2,32]{1,0:T(4,128)(4,1)}, pred[2,32]{1,0:T(4,128)(4,1)S(1)}, u32[]{:S(2)}) copy-start(pred[2,32]{1,0:T(4,128)(4,1)S(1)} %get-tuple-element.99) | copy-start | bytes 196
  100.1 3.6 copy-start.52
  100.1 3.6 copy-start.54
  104.7 5.9 copy-start.61
  130.9 144.0 %all-to-all-start.1 = ((f32[32,2,2,96,128]{4,2,3,1,0:T(2,128)}), f32[32,2,2,96,128]{4,2,3,1,0:T(2,128)}, u32[]{:S(2)}, u32[]{:S(2)}) async-start(f32[32,2,2,96,128]{4,2,3,1,0:T(2,128)} %copy.127), calls=%async_computation.1 | async-start | bytes 12582912 | tf_op jit(solution)/shard_map/all_to_all | solution.py:85
  135.1 5.3 copy-start.24
  278.2 11.5 %copy-start.7 = (f32[32,2,2,32,128]{4,2,3,1,0:T(2,128)}, f32[32,2,2,32,128]{4,2,3,1,0:T(2,128)S(1)}, u32[]{:S(2)}) copy-start(f32[32,2,2,32,128]{4,2,3,1,0:T(2,128)S(1)} %get-tuple-element.26) | copy-start | bytes 6291460
  278.2 19.3 %copy-start.11 = (f32[32,2,2,32,128]{4,2,3,1,0:T(2,128)}, f32[32,2,2,32,128]{4,2,3,1,0:T(2,128)S(1)}, u32[]{:S(2)}) copy-start(f32[32,2,2,32,128]{4,2,3,1,0:T(2,128)S(1)} %get-tuple-element.25) | copy-start | bytes 6291460
  278.2 4.4 copy-start
  303.2 3.7 copy-start.22
  315.2 37.8 %all-to-all-start.2 = ((f32[32,2,2,22,128]{4,2,3,1,0:T(2,128)}), f32[32,2,2,22,128]{4,2,3,1,0:T(2,128)S(1)}, u32[]{:S(2)}, u32[]{:S(2)}) async-start(f32[32,2,2,22,128]{4,2,3,1,0:T(2,128)} %copy.136), calls=%async_computation.2 | async-start | bytes 2883584 | tf_op jit(solution)/shard_map/all_to_all | solution.py:85
  362.5 3.1 copy-start.62
  550.7 3.6 copy-start.25
  554.3 3.9 copy-start.10
  581.5 3.6 copy-start.33
  591.5 5.6 copy-start.67
  591.6 5.6 copy-start.68
  591.6 40.4 %copy-start.38 = (f32[32,2,32,2,1,1]{2,0,3,1,5,4:T(8,128)S(1)}, f32[32,2,32,2,1,1]{2,0,3,1,5,4:T(8,128)}, u32[]{:S(2)}) copy-start(f32[32,2,32,2,1,1]{2,0,3,1,5,4:T(8,128)} %constant.147) | copy-start | bytes 49156
  593.4 39.4 %copy-start.43 = (f32[32,128]{1,0:T(8,128)S(1)}, f32[32,128]{1,0:T(8,128)}, u32[]{:S(2)}) copy-start(f32[32,128]{1,0:T(8,128)} %constant.143) | copy-start | bytes 49156
  593.4 39.4 %copy-start.60 = (f32[32,128]{1,0:T(8,128)S(1)}, f32[32,128]{1,0:T(8,128)}, u32[]{:S(2)}) copy-start(f32[32,128]{1,0:T(8,128)} %constant.144) | copy-start | bytes 49156
  593.4 38.5 %all-to-all-start.4 = ((f32[32,2,2,22,128]{4,2,3,1,0:T(2,128)}), f32[32,2,2,22,128]{4,2,3,1,0:T(2,128)S(1)}, u32[]{:S(2)}, u32[]{:S(2)}) async-start(f32[32,2,2,22,128]{4,2,3,1,0:T(2,128)} %copy.151), calls=%async_computation.4 | async-start | bytes 2883584 | tf_op jit(solution)/shard_map/all_to_all | solution.py:85
  645.3 4.0 copy-start.83
  656.5 97.7 %all-to-all-start.5 = ((f32[32,2,2,2,32,128]{5,4,3,2,1,0:T(8,128)}), f32[32,2,2,2,32,128]{5,4,3,2,1,0:T(8,128)}, u32[]{:S(2)}, u32[]{:S(2)}) async-start(f32[32,2,2,2,32,128]{5,4,3,2,1,0:T(8,128)} %copy.154), calls=%async_computation.5 | async-start | bytes 8388608 | tf_op jit(solution)/shard_map/all_to_all | solution.py:85
  863.3 15.2 %copy-start.40 = (f32[2,256,256]{2,1,0:T(8,128)S(1)}, f32[2,256,256]{2,1,0:T(8,128)}, u32[]{:S(2)}) copy-start(f32[2,256,256]{2,1,0:T(8,128)} %constant.126.clone) | copy-start | bytes 1572868
  (57 other events, 102.1 us)

commit v2 on v1

--- a/solution.py
+++ b/solution.py
@@ -39,21 +39,8 @@
     out = {"A": A, "B": B, "half": half}
     cos_t, sin_t = turn(k[:, None] * a[None, :], A)
     out["y1"] = np.stack([cos_t, -sin_t], 1).astype(np.float32)
-    ky = k[:, None] + A * j[None, :]
-    cos_t, sin_t = turn(ky[:, :, None] * b, grid)
-    y2 = rotation(cos_t * scale, -sin_t * scale, (1, 3))
-    plain = y2.copy()
-    y2[0, 1, 0, 0, :] = scale * (-1.0) ** b
-    y2[0, 1, 0, 1, :] = 0.0
-    out["y2"], out["y2_plain"] = y2, plain
-    weight = np.where(ky == 0, 1.0, 2.0)[:, :, None] * scale
-    cos_t, sin_t, weight = (t.swapaxes(1, 2) for t in (cos_t, sin_t, weight))
-    iy = rotation(cos_t * weight, sin_t * weight, (1, 3))
-    slope = (ky * (2.0 * np.pi / grid))[:, None, :] * weight
-    iyd = rotation(-sin_t * slope, cos_t * slope, (1, 3))
-    iy[0, 0, :, 1, 0] = scale * (-1.0) ** b
-    iy[0, 1, :, 1, 0] = 0.0
-    out["iy"], out["iyd"] = iy, iyd
+    out["kb"] = np.stack(turn(k[:, None] * b[None, :], grid)).astype(np.float32)
+    out["jb"] = np.stack(turn(j[:, None] * b[None, :], B)).astype(np.float32)
     cos_t, sin_t = turn(a[:, None] * k[None, :], A)
     out["iy1"] = np.stack([cos_t, -sin_t], 2).astype(np.float32)
     p, s = np.arange(total), np.arange(total)
@@ -69,11 +56,46 @@
     return out
 
 
+def second_tables(tables, grid):
+    scale = 1.0 / math.sqrt(grid)
+    kb, jb = lax.optimization_barrier((tables["kb"], tables["jb"]))
+    k = lax.broadcasted_iota(jnp.int32, (tables["A"], 1, 1, 1, 1), 0)
+
+    def multiplied(left, right):
+        return (left[0] * right[0] - left[1] * right[1], left[1] * right[0] + left[0] * right[1])
+
+    def paired(cos_part, sin_part):
+        to_real = jnp.stack([cos_part, -sin_part], 2)
+        to_imag = jnp.stack([sin_part, cos_part], 2)
+        return jnp.stack([to_real, to_imag], 1)
+
+    half, width = tables["half"], tables["B"]
+    sign = scale * (1.0 - 2.0 * (lax.iota(jnp.int32, width) % 2).astype(jnp.float32))
+    d = lax.broadcasted_iota(jnp.int32, (1, 2, 1, 1, 1), 1)
+    cos_t, sin_t = multiplied(kb[:, :, None, :], jb[:, None, :, :])
+    plain = paired(scale * cos_t, -scale * sin_t)
+    j = lax.broadcasted_iota(jnp.int32, (1, 1, half, 1, 1), 2)
+    c = lax.broadcasted_iota(jnp.int32, (1, 1, 1, 2, 1), 3)
+    riding = jnp.where(c == 0, sign[None, None, None, None, :], 0.0)
+    table = jnp.where((k == 0) & (d == 1) & (j == 0), riding, plain)
+    cos_t, sin_t = multiplied(kb[:, :, :, None], jb.swapaxes(1, 2)[:, None])
+    ky = k[:, :, :, 0, 0] + tables["A"] * lax.broadcasted_iota(jnp.int32, (1, 1, half), 2)
+    weight = jnp.where(ky == 0, scale, 2.0 * scale)
+    slope = ky.astype(jnp.float32) * (2.0 * math.pi / grid) * weight
+    back = paired(cos_t * weight, sin_t * weight)
+    j = lax.broadcasted_iota(jnp.int32, (1, 1, 1, 1, half), 4)
+    riding = jnp.where(d == 0, sign[None, None, :, None, None], 0.0)
+    back = jnp.where((k == 0) & (c == 1) & (j == 0), riding, back)
+    back_slope = paired(-sin_t * slope, cos_t * slope)
+    return {"y2": table, "y2_plain": plain, "iy": back, "iyd": back_slope}
+
+
 def body(vorticity_grid, forcing_grid, cutoff, forcing_shells):
     rows, grid = vorticity_grid.shape
     total = lax.axis_size("gx") * lax.axis_size("gy")
     rank = lax.axis_index("gx") * lax.axis_size("gy") + lax.axis_index("gy")
     tables = wave_tables(grid, total, rows)
+    tables.update(second_tables(tables, grid))
     A, B, half = tables["A"], tables["B"], tables["half"]
     local = A // total
     half_low = LOW // 2
@@ -263,28 +285,30 @@
         [jnp.broadcast_to(nyquist, flipped[:, :, :, :1].shape), flipped[:, :, :, :-1]], 3
     )
     flipped = jnp.where((k_ids == 0)[:, :, None], shifted, flipped)
+    lanes = np.arange(rows)
+    head_turn = (lanes[:, None] == (rows - lanes[None, :]) % rows).astype(np.float32)
+    tail_turn = (lanes[:, None] == rows - 1 - lanes[None, :]).astype(np.float32)
+    flipped = flipped * jnp.array([1.0, -1.0], jnp.float32)[None, None, :, None, None]
+    highest = lax.Precision.HIGHEST
+    head = jnp.einsum("pkdjq,qr->pkdjr", flipped[:1], head_turn, precision=highest)
+    tail = jnp.einsum("pkdjq,qr->pkdjr", flipped[1:], tail_turn, precision=highest)
+    flipped = jnp.concatenate([head, jnp.flip(tail, 0)], 0)
     whole = jnp.concatenate([straight, flipped], 3)
-    sent = whole.transpose(3, 1, 2, 0, 4)
+    backwards = rank >= total // 2
     if rows >= A:
-        sent = sent.reshape(total, rows // A, local, 2, total, rows)
-        got = exchange(sent)
-        sources = got.reshape(total, rows // A, local, 2, total, rows)
-        placed = sources.transpose(3, 1, 0, 2, 5, 4).reshape(2, rows, grid)
-        back = jnp.roll(
-            jnp.flip(placed.reshape(2, rows // A, A, grid), 2), 1, 2
-        ).reshape(2, rows, grid)
+        shape = (total, local, 2, total, rows // A, rows)
+        sent = whole.reshape(shape).transpose(3, 1, 4, 2, 0, 5)
+        block = exchange(sent).reshape(A, rows // A, 2, total, rows)
+        block = jnp.where(backwards, jnp.roll(jnp.flip(block, 0), 1, 0), block)
+        spectrum = block.transpose(2, 1, 0, 4, 3).reshape(2, rows, grid)
     else:
         parts = A // rows
+        sent = whole.transpose(3, 1, 2, 0, 4)
         sent = jnp.broadcast_to(sent[:, None], (B, parts) + sent.shape[1:])
         block = exchange(sent.reshape((total,) + sent.shape[2:])).reshape(A, 2, total, rows)
-        block = block.transpose(1, 0, 3, 2).reshape(2, A, grid)
-        start = (rank % parts) * rows
-        placed = lax.dynamic_slice_in_dim(block, start, rows, 1)
-        turned_block = jnp.roll(jnp.flip(block, 1), 1, 1)
-        back = lax.dynamic_slice_in_dim(turned_block, start, rows, 1)
-    back = mirrored(back)
-    back = jnp.stack([back[0], -back[1]])
-    spectrum = jnp.where(rank >= total // 2, back, placed)
+        block = jnp.where(backwards, jnp.roll(jnp.flip(block, 0), 1, 0), block)
+        block = lax.dynamic_slice_in_dim(block, (rank % parts) * rows, rows, 0)
+        spectrum = block.transpose(1, 0, 3, 2).reshape(2, rows, grid)
 
     own = LOW // total
     block_ids = np.arange(LOW)

time: 894 us -> 832 us (0.931)
  local copies, waits for them, and re-layouts: 180 us -> 114 us
    unnamed x184 -> x209, local copies, waits for them, and re-layouts: 67.2 us -> 33.5 us
    slice x3, local copies, waits for them, and re-layouts: 24 us -> 10.8 us  [body(): block = jnp.where(backwards, jnp.roll(jnp.flip(block, 0), 1, 0), block)]
    another operation x1 -> x0, local copies, waits for them, and re-layouts: 13 us -> none  [body(): placed.reshape(2, rows // A, A, grid)]
  transfers between devices with their start and end apart: 5 -> 5, of which waited for: 5 -> 5; matrix products, arithmetic and copies ran while one was open for 2% -> 3% of each run, Pallas kernels for 0% -> 0%
where the time goes in v2:
time: 832 us; the launch traced here: 821 us
  waiting for transfers between devices  325 us (39%)
  blocking collectives  174 us (21%)
  matrix products  131 us (16%)
  local copies, waits for them, and re-layouts  114 us (14%)
  other arithmetic  45.1 us (5%)
  starting transfers between devices  22.3 us (3%)
  between operations  10.5 us (1%)
    all_to_all x5, waiting for transfers between devices, exchange(): return lax.all_to_all(values, AXES, split_axis=0, concat_axis=0, tiled=True)  325 us
    all_to_all x2, blocking collectives, exchange(): return lax.all_to_all(values, AXES, split_axis=0, concat_axis=0, tiled=True)  174 us
    dot_general x36, matrix products, contract(): jnp.einsum(pattern, left_side, right_side, precision=lax.Precision.HIGH)  128 us
    unnamed x209, local copies, waits for them, and re-layouts  33.5 us
    all_to_all x5, starting transfers between devices, exchange(): return lax.all_to_all(values, AXES, split_axis=0, concat_axis=0, tiled=True)  22.3 us
    transpose x3, local copies, waits for them, and re-layouts, contract(): jnp.einsum(pattern, left_side, right_side, precision=lax.Precision.HIGH)  19 us
  transfers between devices with their start and end apart: 5, of which 5 were waited for; matrix products, arithmetic and copies ran while one was open for 3% of the time, Pallas kernels for 0%

profile of v2, /device:TPU:0, one launch (start us, length us, event | category | flops | bytes accessed | tf_op | source)
XLA Modules:
  0.0 820.7 jit_solution(10306292651187544082)
XLA Ops:
  7.0 4.5 convolution_bitcast_fusion.7
  19.8 5.4 fusion.9
  29.0 7.3 all-to-all-start
  37.8 50.1 %all-to-all-done = f32[32,2,2,34,128]{4,2,3,1,0:T(2,128)S(1)} async-done(((f32[32,2,2,34,128]{4,2,3,1,0:T(2,128)}), f32[32,2,2,34,128]{4,2,3,1,0:T(2,128)S(1)}, u32[]{:S(2)}, u32[]{:S(2)}) %all-to-all-start) | async-done | bytes 2228256 | tf_op jit(solution)/shard_map/all_to_all | solution.py:107
  106.4 5.9 fusion.50
  114.4 6.9 fusion.53
  121.3 7.5 copy.139
  128.8 4.4 all-to-all-start.1
  141.1 4.9 fusion.27
  146.1 127.0 %all-to-all-done.1 = f32[32,2,2,96,128]{4,2,3,1,0:T(2,128)} async-done(((f32[32,2,2,96,128]{4,2,3,1,0:T(2,128)}), f32[32,2,2,96,128]{4,2,3,1,0:T(2,128)}, u32[]{:S(2)}, u32[]{:S(2)}) %all-to-all-start.1) | async-done | bytes 6291488 | tf_op jit(solution)/shard_map/all_to_all | solution.py:107
  289.1 4.2 fusion.60
  293.3 4.1 fusion.31
  297.7 4.2 fusion.63
  307.8 4.4 fusion.14
  332.6 19.2 %all-to-all-done.2 = f32[32,2,2,22,128]{4,2,3,1,0:T(2,128)S(1)} async-done(((f32[32,2,2,22,128]{4,2,3,1,0:T(2,128)}), f32[32,2,2,22,128]{4,2,3,1,0:T(2,128)S(1)}, u32[]{:S(2)}, u32[]{:S(2)}) %all-to-all-start.2) | async-done | bytes 1441824 | tf_op jit(solution)/shard_map/all_to_all | solution.py:107
  366.4 8.7 %fusion.47 = f32[32,2,2,108,128]{4,0,2,3,1:T(8,128)} fusion(f32[32,2,32,2,1,1]{2,0,3,1,5,4:T(8,128)S(1)} %copy-done.55, f32[32,2,2,108,128,1]{4,3,2,1,0,5:T(8,128)S(1)} %maximum_bitcast_fusion.1), kind=kOutput, calls=%fused_computation.62 | convolution fusion | flops 679477248 | bytes 14172160 | tf_op jit(solution)/shard_map/sdpc,pkcjl->skdjl/dot_general | solution.py:19
  375.2 11.3 %copy.155 = f32[32,2,2,108,128]{4,2,3,1,0:T(2,128)} copy(f32[32,2,2,108,128]{4,0,2,3,1:T(8,128)} %fusion.47) | data formatting | bytes 14155776 | tf_op jit(solution)/shard_map/sdpc,pkcjl->skdjl/transpose | solution.py:19
  386.5 159.0 %all_to_all.35 = f32[32,2,2,108,128]{4,2,3,1,0:T(2,128)S(1)} all-to-all(f32[32,2,2,108,128]{4,2,3,1,0:T(2,128)} %copy.155), channel_id=1, replica_groups=mesh['gx'=8,'gy'=4] {'gx','gy'}, dimensions={0} | all-to-all | bytes 14155776 | tf_op jit(solution)/shard_map/all_to_all | solution.py:107
  559.5 4.4 fusion.66
  569.8 4.2 fusion.69
  573.9 4.1 fusion.21
  587.8 4.6 fusion.12
  598.1 34.8 %all-to-all-done.4 = f32[32,2,2,22,128]{4,2,3,1,0:T(2,128)S(1)} async-done(((f32[32,2,2,22,128]{4,2,3,1,0:T(2,128)}), f32[32,2,2,22,128]{4,2,3,1,0:T(2,128)S(1)}, u32[]{:S(2)}, u32[]{:S(2)}) %all-to-all-start.4) | async-done | bytes 1441824 | tf_op jit(solution)/shard_map/all_to_all | solution.py:107
  660.0 4.4 copy.399
  668.5 93.7 %all-to-all-done.5 = f32[32,2,2,2,32,128]{5,4,3,2,1,0:T(8,128)} async-done(((f32[32,2,2,2,32,128]{5,4,3,2,1,0:T(8,128)}), f32[32,2,2,2,32,128]{5,4,3,2,1,0:T(8,128)}, u32[]{:S(2)}, u32[]{:S(2)}) %all-to-all-start.5) | async-done | bytes 4194336 | tf_op jit(solution)/shard_map/all_to_all | solution.py:107
  762.2 5.0 slice.308
  768.0 5.0 slice.258
  773.0 6.9 fusion.11
  779.9 9.0 %copy.175 = f32[2,2,64,128,32]{2,1,4,3,0:T(2,128)} copy(f32[2,2,64,128,32]{3,4,0,1,2:T(8,128)} %fusion.11) | data formatting | bytes 8388608 | tf_op jit(solution)/shard_map/transpose | solution.py:303
  788.9 8.8 %reshape.926 = f32[2,128,4096]{1,2,0:T(8,128)} reshape(f32[2,2,64,128,32]{2,1,4,3,0:T(2,128)} %copy.175) | data formatting | bytes 8388608 | tf_op jit(solution)/shard_map/reshape | solution.py:303
  797.7 5.7 copy.181
  805.1 14.5 %all_to_all.36 = f32[32,2,128,8]{2,3,1,0:T(8,128)S(1)} all-to-all(f32[32,2,128,8]{2,3,1,0:T(8,128)S(1)} %copy.179), channel_id=1, replica_groups=mesh['gx'=8,'gy'=4] {'gx','gy'}, dimensions={0} | all-to-all | bytes 524288 | tf_op jit(solution)/shard_map/all_to_all | solution.py:107
  (327 shorter events, 166.0 us)
Async XLA Ops:
  14.7 283.0 %copy-start.37 = (pred[64,2,32]{2,1,0:T(4,128)(4,1)}, pred[64,2,32]{2,1,0:T(4,128)(4,1)S(1)}, u32[]{:S(2)}) copy-start(pred[64,2,32]{2,1,0:T(4,128)(4,1)S(1)} %broadcast_and_fusion) | copy-start | bytes 12292
  14.7 282.9 %copy-start.84 = (f32[2,64]{1,0:T(2,128)}, f32[2,64]{1,0:T(2,128)S(1)}, u32[]{:S(2)}) copy-start(f32[2,64]{1,0:T(2,128)S(1)} %broadcast_select_fusion) | copy-start | bytes 1540
  15.7 4.1 copy-start.3
  15.7 4.1 copy-start.6
  29.0 58.9 %copy-start.45 = (f32[32,2,32,2,1,1]{2,0,3,1,5,4:T(8,128)S(1)}, f32[32,2,32,2,1,1]{2,0,3,1,5,4:T(8,128)}, u32[]{:S(2)}) copy-start(f32[32,2,32,2,1,1]{2,0,3,1,5,4:T(8,128)} %constant.184) | copy-start | bytes 49156
  29.0 58.9 %all-to-all-start = ((f32[32,2,2,34,128]{4,2,3,1,0:T(2,128)}), f32[32,2,2,34,128]{4,2,3,1,0:T(2,128)S(1)}, u32[]{:S(2)}, u32[]{:S(2)}) async-start(f32[32,2,2,34,128]{4,2,3,1,0:T(2,128)} %copy.122), calls=%async_computation | async-start | bytes 4456448 | tf_op jit(solution)/shard_map/all_to_all | solution.py:107
  37.0 65.9 %copy-start.88 = (s32[128]{0:T(128)}, s32[128]{0:T(128)S(1)}, u32[]{:S(2)}) copy-start(s32[128]{0:T(128)S(1)} %iota_multiply_fusion.1) | copy-start | bytes 1540
  37.0 50.9 %copy-start.94 = (pred[2]{0:T(512)(128)(4,1)}, pred[2]{0:T(512)(128)(4,1)S(1)}, u32[]{:S(2)}) copy-start(pred[2]{0:T(512)(128)(4,1)S(1)} %broadcast_compare_fusion) | copy-start | bytes 10
  37.1 66.4 %copy-start.82 = (s32[2,32]{1,0:T(2,128)}, s32[2,32]{1,0:T(2,128)S(1)}, u32[]{:S(2)}) copy-start(s32[2,32]{1,0:T(2,128)S(1)} %add_multiply_fusion.3) | copy-start | bytes 772
  37.8 65.7 %copy-start.86 = (pred[2,32]{1,0:T(4,128)(4,1)}, pred[2,32]{1,0:T(4,128)(4,1)S(1)}, u32[]{:S(2)}) copy-start(pred[2,32]{1,0:T(4,128)(4,1)S(1)} %get-tuple-element.131) | copy-start | bytes 196
  106.4 5.9 copy-start.70
  128.8 4.4 copy-start.68
  128.8 144.2 %all-to-all-start.1 = ((f32[32,2,2,96,128]{4,2,3,1,0:T(2,128)}), f32[32,2,2,96,128]{4,2,3,1,0:T(2,128)}, u32[]{:S(2)}, u32[]{:S(2)}) async-start(f32[32,2,2,96,128]{4,2,3,1,0:T(2,128)} %copy.139), calls=%async_computation.1 | async-start | bytes 12582912 | tf_op jit(solution)/shard_map/all_to_all | solution.py:107
  137.6 3.6 copy-start.32
  276.4 6.8 copy-start.23
  276.4 10.5 %copy-start.19 = (f32[32,2,2,32,128]{4,2,3,1,0:T(2,128)}, f32[32,2,2,32,128]{4,2,3,1,0:T(2,128)S(1)}, u32[]{:S(2)}) copy-start(f32[32,2,2,32,128]{4,2,3,1,0:T(2,128)S(1)} %get-tuple-element.34) | copy-start | bytes 6291460
  276.4 21.0 %copy-start.21 = (f32[32,2,2,32,128]{4,2,3,1,0:T(2,128)}, f32[32,2,2,32,128]{4,2,3,1,0:T(2,128)S(1)}, u32[]{:S(2)}) copy-start(f32[32,2,2,32,128]{4,2,3,1,0:T(2,128)S(1)} %get-tuple-element.35) | copy-start | bytes 6291460
  301.8 3.7 copy-start.31
  314.0 37.8 %all-to-all-start.2 = ((f32[32,2,2,22,128]{4,2,3,1,0:T(2,128)}), f32[32,2,2,22,128]{4,2,3,1,0:T(2,128)S(1)}, u32[]{:S(2)}, u32[]{:S(2)}) async-start(f32[32,2,2,22,128]{4,2,3,1,0:T(2,128)} %copy.150), calls=%async_computation.2 | async-start | bytes 2883584 | tf_op jit(solution)/shard_map/all_to_all | solution.py:107
  549.4 3.6 copy-start.33
  563.9 3.9 copy-start.22
  581.9 3.7 copy-start.41
  594.3 3.7 copy-start.77
  594.3 3.8 copy-start.78
  594.3 38.6 %copy-start.46 = (f32[32,2,32,2,1,1]{2,0,3,1,5,4:T(8,128)S(1)}, f32[32,2,32,2,1,1]{2,0,3,1,5,4:T(8,128)}, u32[]{:S(2)}) copy-start(f32[32,2,32,2,1,1]{2,0,3,1,5,4:T(8,128)} %constant.184) | copy-start | bytes 49156
  594.3 38.5 %all-to-all-start.4 = ((f32[32,2,2,22,128]{4,2,3,1,0:T(2,128)}), f32[32,2,2,22,128]{4,2,3,1,0:T(2,128)S(1)}, u32[]{:S(2)}, u32[]{:S(2)}) async-start(f32[32,2,2,22,128]{4,2,3,1,0:T(2,128)} %copy.167), calls=%async_computation.4 | async-start | bytes 2883584 | tf_op jit(solution)/shard_map/all_to_all | solution.py:107
  598.0 35.7 %copy-start.51 = (f32[32,128]{1,0:T(8,128)S(1)}, f32[32,128]{1,0:T(8,128)}, u32[]{:S(2)}) copy-start(f32[32,128]{1,0:T(8,128)} %constant.180) | copy-start | bytes 49156
  598.0 35.7 %copy-start.67 = (f32[32,128]{1,0:T(8,128)S(1)}, f32[32,128]{1,0:T(8,128)}, u32[]{:S(2)}) copy-start(f32[32,128]{1,0:T(8,128)} %constant.181) | copy-start | bytes 49156
  654.4 3.2 copy-start.76
  664.5 97.7 %all-to-all-start.5 = ((f32[32,2,2,2,32,128]{5,4,3,2,1,0:T(8,128)}), f32[32,2,2,2,32,128]{5,4,3,2,1,0:T(8,128)}, u32[]{:S(2)}, u32[]{:S(2)}) async-start(f32[32,2,2,2,32,128]{5,4,3,2,1,0:T(8,128)} %bitcast.503), calls=%async_computation.5 | async-start | bytes 8388608 | tf_op jit(solution)/shard_map/all_to_all | solution.py:107
  797.7 6.7 copy-start.42
  803.4 16.2 %copy-start.48 = (f32[2,256,256]{2,1,0:T(8,128)S(1)}, f32[2,256,256]{2,1,0:T(8,128)}, u32[]{:S(2)}) copy-start(f32[2,256,256]{2,1,0:T(8,128)} %constant.163.clone) | copy-start | bytes 1572868
  (70 other events, 119.9 us)
